TPU v7x, 32 devices: a whole 2x2x4 slice. The times are simulated.
32 devices in a mesh: pts: 4 (over y, x), lmk: 8 (over z, core).
Axes of the slice: x: 2, y: 2, z: 4, core: 2. Of those that a mesh axis runs over, the one named last changes fastest.
Arguments:
- points: float32 [16384, 384], P('pts'), may hold values from -8 to 8
- labels: int32 [16384], P('pts'), may hold values from 0 to 127
- landmarks: float32 [16384, 384], P('lmk'), may hold values from -8 to 8
- coefficients: float32 [16384, 128], P('lmk'), may hold values from -4 to 4
Outputs:
- gradient: float32 [16384, 128], P('lmk')
All inputs are finite; a program needn't handle non-finite values.
Results may differ from a plain program's by a relative error of at most 0.0003.
Values sent between devices are 32-bit elements; how exact they have to be, the bound alone decides.
A program may use at most 128 MiB of HBM per device.

v0:
```python
import jax
import jax.numpy as jnp
from jax import lax
from jax.sharding import PartitionSpec as P

LOSS_SCALE = 8192.0
RIDGE = 0.5


def residual_rows(logits, labels):
    classes = logits.shape[1]
    expo = jnp.exp(logits)
    onehot = (labels[:, None] == jnp.arange(classes, dtype=jnp.int32)[None, :]).astype(jnp.float32)
    return expo / jnp.sum(expo, axis=1, keepdims=True) - onehot


def per_device(points, labels, landmarks, coefficients):
    high = lax.Precision.HIGHEST
    feats = points.shape[1]
    pnorm = jnp.sum(points * points, axis=1)
    lnorm = jnp.sum(landmarks * landmarks, axis=1)
    cross = jnp.dot(points, landmarks.T, precision=high, preferred_element_type=jnp.float32)
    kernel = jnp.exp(-(pnorm[:, None] + lnorm[None, :] - 2.0 * cross) / feats)
    partial_logits = jnp.dot(
        kernel, coefficients, precision=high, preferred_element_type=jnp.float32
    )
    logits = lax.psum(partial_logits, "lmk")
    resid = residual_rows(logits, labels)
    local_terms = lax.dot_general(
        kernel, resid, (((0,), (0,)), ((), ())), precision=high, preferred_element_type=jnp.float32
    )
    summed = lax.psum(local_terms, "pts")
    total_points = labels.shape[0] * lax.axis_size("pts")
    return summed * (LOSS_SCALE / total_points) + RIDGE * coefficients


def solution(mesh):
    in_specs = (P("pts", None), P("pts"), P("lmk", None), P("lmk", None))
    out_specs = P("lmk", None)
    return jax.shard_map(
        per_device, mesh=mesh, in_specs=in_specs, out_specs=out_specs, check_vma=False
    )
```

profile of v0, /device:TPU:0, one launch (start us, length us, event | category | flops | bytes accessed | tf_op | source)
XLA Modules:
  0.0 299.8 jit_solution(14387722691670884355)
XLA Ops:
  6.5 0.0 copy-start
  6.5 0.0 all-reduce.3.cloned.1.call-start
  6.5 2.3 multiply_reduce_fusion.1
  8.9 3.4 %multiply_reduce_fusion = f32[4096]{0:T(1024)S(1)} fusion(f32[4096,384]{1,0:T(8,128)} %param.4), kind=kLoop, calls=%fused_computation.11 | loop fusion | flops 3141632 | bytes 6307840 | tf_op jit(solution)/shard_map/reduce_sum | solution.py:20
  12.3 58.6 %fusion.20 = f32[4096,2048]{1,0:T(8,128)} fusion(f32[4096,384]{1,0:T(8,128)} %param.4, f32[2048,384]{1,0:T(8,128)} %param.6), kind=kOutput, calls=%fused_computation.26 | convolution fusion | flops 38654705664 | bytes 42991616 | tf_op jit(solution)/shard_map/dot_general | solution.py:22
  70.9 0.0 copy-done
  70.9 0.0 copy-start.1
  70.9 35.0 %fusion.1 = f32[4096,128]{1,0:T(8,128)} fusion(f32[2048,128]{1,0:T(8,128)S(1)} %copy-done, f32[4096,2048]{1,0:T(8,128)} %fusion.20, f32[2048]{0:T(1024)S(1)} %multiply_reduce_fusion.1, f32[4096]{0:T(1024)S(1)} %multiply_reduce_fusion), kind=kOutput, calls=%fused_computation.2 | convolution fusion | flops 12926844928 | bytes 36724736 | tf_op jit(solution)/shard_map/dot_general | solution.py:24
  105.8 0.0 all-reduce.3.cloned.1.call-update
  105.8 0.0 all-reduce.5.cloned.1.call-start
  105.9 68.0 %all-reduce.3.cloned.1.call-done = f32[4096,128]{1,0:T(8,128)} async-done(((f32[4096,128]{1,0:T(8,128)}), f32[4096,128]{1,0:T(8,128)}) %all-reduce.3.cloned.1.call-update) | async-done | bytes 2097168 | tf_op jit(solution)/shard_map/psum | solution.py:27
  173.9 2.2 exponential_reduce_fusion
  176.1 0.0 copy-done.1
  176.1 62.3 %fusion = f32[2048,128]{1,0:T(8,128)} fusion(f32[4096,2048]{1,0:T(8,128)} %fusion.20, f32[2048]{0:T(1024)S(1)} %multiply_reduce_fusion.1, f32[4096]{0:T(1024)S(1)} %multiply_reduce_fusion, f32[4096,128]{1,0:T(8,128)} %all-reduce.3.cloned.1.call-done, s32[4096]{0:T(1024)S(1)} %copy-done.1, f32[4096]{0:T(1024)S(1)} %exponential_reduce_fusion), kind=kOutput, calls=%fused_computation.1 | convolution fusion | flops 12928942080 | bytes 36757504 | tf_op jit(solution)/shard_map/dot_general | solution.py:29
  238.4 0.0 all-reduce.5.cloned.1.call-update
  238.4 52.2 %all-reduce.5.cloned.1.call-done = f32[2048,128]{1,0:T(8,128)} async-done(((f32[2048,128]{1,0:T(8,128)}), f32[2048,128]{1,0:T(8,128)}) %all-reduce.5.cloned.1.call-update) | async-done | bytes 1048592 | tf_op jit(solution)/shard_map/psum | solution.py:32
  290.6 2.3 add_multiply_fusion
Async XLA Ops:
  6.5 64.3 %copy-start = (f32[2048,128]{1,0:T(8,128)S(1)}, f32[2048,128]{1,0:T(8,128)}, u32[]{:S(2)}) copy-start(f32[2048,128]{1,0:T(8,128)} %param.7) | copy-start | bytes 3145732
  6.5 167.4 %all-reduce.3.cloned.1.call-start = ((), (), s32[]{:S(2)}) async-start(), calls=%async_computation | async-start | bytes 4194304 | tf_op jit(solution)/shard_map/psum | solution.py:27
  70.9 105.3 %copy-start.1 = (s32[4096]{0:T(1024)S(1)}, s32[4096]{0:T(1024)}, u32[]{:S(2)}) copy-start(s32[4096]{0:T(1024)} %param.5) | copy-start | bytes 49156
  105.8 184.8 %all-reduce.5.cloned.1.call-start = ((), (), s32[]{:S(2)}) async-start(), calls=%async_computation.1 | async-start | bytes 2097152 | tf_op jit(solution)/shard_map/psum | solution.py:32
Sparse Core Ops, SparseCore 0:
  106.0 67.8 all-reduce.2
  238.5 52.0 all-reduce.4
where the time goes:
time: 300 us
  matrix products  156 us (52%)
  waiting for transfers between devices  120 us (40%)
  between operations  13.4 us (4%)
  other arithmetic  10.2 us (3%)
    psum x1, waiting for transfers between devices, per_device(): logits = lax.psum(partial_logits, 'lmk')  68 us
    dot_general x1, matrix products, per_device(): lax.dot_general(kernel, resid, (((0,), (0,)), ((), ())), precision=high,...  62.3 us
    dot_general x1, matrix products, per_device(): jnp.dot(points, landmarks.T, precision=high, preferred_element_type=jnp.f...  58.6 us
    psum x1, waiting for transfers between devices, per_device(): summed = lax.psum(local_terms, 'pts')  52.2 us
    dot_general x1, matrix products, per_device(): jnp.dot(kernel, coefficients, precision=high, preferred_element_type=jnp....  35 us
  transfers between devices with their start and end apart: 2, of which 2 were waited for; matrix products, arithmetic and copies ran while one was open for 0% of the time, Pallas kernels for 0%

commit v1 on v0

v1 whole, which is shorter than its diff:
```python
import functools

import jax
import jax.numpy as jnp
from jax import lax
from jax.experimental import pallas as pl
from jax.experimental.pallas import tpu as pltpu
from jax.sharding import PartitionSpec as P

LOSS_SCALE = 8192.0
RIDGE = 0.5
LOG2E = 1.4426950408889634
BF = jnp.bfloat16
F32 = jnp.float32


def halves(x):
    hi = x.astype(BF)
    return hi, (x - hi.astype(F32)).astype(BF)


def dot(a, b):
    return jnp.dot(a, b, preferred_element_type=F32)


def dot_nt(a, b):
    return lax.dot_general(a, b, (((1,), (1,)), ((), ())), preferred_element_type=F32)


def extra_columns(norm, first):
    n1 = norm.astype(BF).astype(F32)
    n2 = (norm - n1).astype(BF).astype(F32)
    n3 = ((norm - n1) - n2).astype(BF).astype(F32)
    lane = lax.broadcasted_iota(jnp.int32, (norm.shape[0], 128), 1)
    ones = jnp.where((lane >= 3 - first) & (lane < 6 - first), 1.0, 0.0)
    ext = jnp.where(lane == first, n1, ones)
    ext = jnp.where(lane == first + 1, n2, ext)
    return jnp.where(lane == first + 2, n3, ext).astype(BF)


def body(cfg, pts_ref, lab_ref, lmk_ref, coef_ref, out_ref,
         ls, cc, ps, kh, kl, logit, prob, recv, acc, grecv,
         send_sem, recv_sem, gsend, grecv_sem):
    rows, tile, npts, nlmk, scale = cfg
    n, feats = pts_ref.shape
    m, classes = coef_ref.shape
    chunks = n // rows
    lbits, pbits = nlmk.bit_length() - 1, npts.bit_length() - 1
    stages = 2 * lbits
    my_l, my_p = lax.axis_index("lmk"), lax.axis_index("pts")

    barrier = pltpu.get_barrier_semaphore()
    for b in range(lbits):
        pl.semaphore_signal(barrier, inc=1, device_id={"lmk": my_l ^ (1 << b)},
                            device_id_type=pl.DeviceIdType.MESH)
    for b in range(pbits):
        pl.semaphore_signal(barrier, inc=1, device_id={"pts": my_p ^ (1 << b)},
                            device_id_type=pl.DeviceIdType.MESH)
    pl.semaphore_wait(barrier, lbits + pbits)

    def split_landmarks(i, _):
        r = pl.ds(pl.multiple_of(i * tile, tile), tile)
        x = lmk_ref[r, :]
        hi, lo = halves(x * (2.0 * LOG2E / feats))
        ls[r, :feats] = hi
        ls[r, feats:2 * feats] = hi
        ls[r, 2 * feats:3 * feats] = lo
        norm = jnp.sum(x * x, axis=1, keepdims=True) * (-LOG2E / feats)
        ls[r, 3 * feats:] = extra_columns(norm, 3)
        hi, lo = halves(coef_ref[r, :])
        cc[r, :classes] = hi
        cc[r, classes:] = lo
        return 0

    lax.fori_loop(0, m // tile, split_landmarks, 0)
    acc[...] = jnp.zeros_like(acc)

    def region(me, bits, total):
        offset, size = 0, total
        for b in bits:
            size //= 2
            offset = offset + ((me >> b) & 1) * size
        return offset, size

    order = list(range(lbits))
    recv_base = [rows - (rows >> s) for s in range(lbits)]

    def exchange(s, chunk):
        base = chunk * rows
        if s < lbits:
            b = order[s]
            at, size = region(my_l, order[:s], rows)
            size //= 2
            other = 1 - ((my_l >> b) & 1)
            src = logit.at[pl.ds(pl.multiple_of(base + at + other * size, 8), size), :]
            dst = recv.at[chunk, pl.ds(recv_base[s], size), :]
        else:
            d = stages - 1 - s
            b = order[d]
            at, size = region(my_l, order[:d + 1], rows)
            src = prob.at[pl.ds(pl.multiple_of(base + at, 8), size), :]
            dst = src
        return pltpu.make_async_remote_copy(
            src_ref=src, dst_ref=dst, send_sem=send_sem.at[s, chunk],
            recv_sem=recv_sem.at[s, chunk], device_id={"lmk": my_l ^ (1 << b)},
            device_id_type=pl.DeviceIdType.MESH)

    def finish(s, chunk):
        exchange(s, chunk).wait()
        if s < lbits:
            at, size = region(my_l, order[:s + 1], rows)
            here = pl.ds(pl.multiple_of(chunk * rows + at, 8), size)
            total = logit[here, :] + recv[chunk, pl.ds(recv_base[s], size), :]
            if s == lbits - 1:
                expo = jnp.exp(total - jnp.max(total, axis=1, keepdims=True))
                prob[here, :] = expo / jnp.sum(expo, axis=1, keepdims=True)
            else:
                logit[here, :] = total

    def forward(chunk):
        r = pl.ds(pl.multiple_of(chunk * rows, rows), rows)
        x = pts_ref[r, :]
        hi, lo = halves(x)
        ps[:, :feats] = hi
        ps[:, feats:2 * feats] = lo
        ps[:, 2 * feats:3 * feats] = hi
        norm = jnp.sum(x * x, axis=1, keepdims=True) * (-LOG2E / feats)
        ps[:, 3 * feats:] = extra_columns(norm, 0)
        total = None
        for j in range(m // tile):
            c = slice(j * tile, (j + 1) * tile)
            k = jnp.exp2(dot_nt(ps[...], ls[c, :]))
            hi, lo = halves(k)
            kh[r, c] = hi
            kl[r, c] = lo
            both = dot(hi, cc[c, :])
            term = both[:, :classes] + both[:, classes:] + dot(lo, cc[c, :classes])
            total = term if total is None else total + term
        logit[r, :] = total

    def backward(chunk):
        r = pl.ds(pl.multiple_of(chunk * rows, rows), rows)
        probs = prob[r, :].T
        labels = lab_ref[:, r]
        classes_at = lax.broadcasted_iota(jnp.int32, (classes, rows), 0)
        resid = probs - jnp.where(classes_at == labels, 1.0, 0.0)
        hi, lo = halves(resid)
        both = jnp.concatenate([hi, lo], axis=0)
        for j in range(m // tile):
            c = slice(j * tile, (j + 1) * tile)
            g = dot(both, kh[r, c])
            acc[:, c] += g[:classes] + g[classes:] + dot(hi, kl[r, c])

    start_back = max(chunks, stages + 1)

    def step(t, _):
        for s in range(stages, -1, -1):
            chunk = t - 1 - s

            @pl.when((chunk >= 0) & (chunk < chunks))
            def _():
                if s > 0:
                    finish(s - 1, chunk)
                if s < stages:
                    exchange(s, chunk).start()

        @pl.when(t < chunks)
        def _():
            forward(t)

        @pl.when(t >= start_back)
        def _():
            backward(t - start_back)

        return 0

    lax.fori_loop(0, start_back + chunks, step, 0)

    for j in range(m // tile):
        c = slice(j * tile, (j + 1) * tile)
        logit[c, :] = acc[:, c].T

    half = m // 2
    orders = [list(range(pbits)), list(range(pbits))[::-1]]
    gbase = [half - (half >> s) for s in range(pbits)]

    def gexchange(h, s):
        base = h * half
        if s < pbits:
            b = orders[h][s]
            at, size = region(my_p, orders[h][:s], half)
            size //= 2
            other = 1 - ((my_p >> b) & 1)
            src = logit.at[pl.ds(pl.multiple_of(base + at + other * size, 8), size), :]
            dst = grecv.at[h, pl.ds(gbase[s], size), :]
        else:
            d = 2 * pbits - 1 - s
            b = orders[h][d]
            at, size = region(my_p, orders[h][:d + 1], half)
            src = out_ref.at[pl.ds(pl.multiple_of(base + at, 8), size), :]
            dst = src
        return pltpu.make_async_remote_copy(
            src_ref=src, dst_ref=dst, send_sem=gsend.at[h, s],
            recv_sem=grecv_sem.at[h, s], device_id={"pts": my_p ^ (1 << b)},
            device_id_type=pl.DeviceIdType.MESH)

    for s in range(2 * pbits + 1):
        for h in range(2):
            if s > 0:
                gexchange(h, s - 1).wait()
                if s - 1 < pbits:
                    at, size = region(my_p, orders[h][:s], half)
                    here = pl.ds(pl.multiple_of(h * half + at, 8), size)
                    total = logit[here, :] + grecv[h, pl.ds(gbase[s - 1], size), :]
                    if s == pbits:
                        out_ref[here, :] = total * scale + RIDGE * coef_ref[here, :]
                    else:
                        logit[here, :] = total
            if s < 2 * pbits:
                gexchange(h, s).start()


def per_device(points, labels, landmarks, coefficients):
    npts, nlmk = lax.axis_size("pts"), lax.axis_size("lmk")
    n, feats = points.shape
    m, classes = coefficients.shape
    rows, tile = 512, 512
    chunks = n // rows
    wide = 3 * feats + 128
    stages = 2 * (nlmk.bit_length() - 1)
    gstages = 2 * (npts.bit_length() - 1)
    cfg = (rows, tile, npts, nlmk, LOSS_SCALE / (n * npts))
    vmem = pl.BlockSpec(memory_space=pltpu.VMEM)
    dma = pltpu.SemaphoreType.DMA
    return pl.pallas_call(
        functools.partial(body, cfg),
        out_shape=jax.ShapeDtypeStruct((m, classes), F32),
        in_specs=[vmem] * 4,
        out_specs=vmem,
        scratch_shapes=[
            pltpu.VMEM((m, wide), BF),
            pltpu.VMEM((m, 2 * classes), BF),
            pltpu.VMEM((rows, wide), BF),
            pltpu.VMEM((n, m), BF),
            pltpu.VMEM((n, m), BF),
            pltpu.VMEM((max(n, m), classes), F32),
            pltpu.VMEM((n, classes), F32),
            pltpu.VMEM((chunks, rows, classes), F32),
            pltpu.VMEM((classes, m), F32),
            pltpu.VMEM((2, m // 2, classes), F32),
            dma((stages, chunks)),
            dma((stages, chunks)),
            dma((2, gstages)),
            dma((2, gstages)),
        ],
        compiler_params=pltpu.CompilerParams(
            collective_id=0, has_side_effects=True, vmem_limit_bytes=67043328),
    )(points, labels.reshape(1, n), landmarks, coefficients)


def solution(mesh):
    in_specs = (P("pts", None), P("pts"), P("lmk", None), P("lmk", None))
    return jax.shard_map(
        per_device, mesh=mesh, in_specs=in_specs, out_specs=P("lmk", None), check_vma=False
    )
```

time: 300 us -> 98.2 us (0.33)
  matrix products: 156 us -> 0 us
  waiting for transfers between devices: 120 us -> 0 us
  Pallas kernels: 0 us -> 95.8 us
  between operations: 13.4 us -> 0.01 us
  other arithmetic: 10.2 us -> 0 us
    dot_general x3 -> x0, matrix products: 156 us -> none  [the longest x1 62.3 us: per_device(): lax.dot_general(kernel, resid, (((0,), (0,)), ((), ())), precision=high,...]
    psum x2 -> x0, waiting for transfers between devices: 120 us -> none  [the longest x1 68 us: per_device(): logits = lax.psum(partial_logits, 'lmk')]
    pallas_call x0 -> x1, Pallas kernels: none -> 95.8 us  [per_device(): pl.pallas_call(functools.partial(body, cfg), out_shape=jax.ShapeDtypeStru...]
    reduce_sum x3 -> x0, other arithmetic: 7.93 us -> none  [the longest x1 3.4 us: per_device(): pnorm = jnp.sum(points * points, axis=1)]
  transfers between devices with their start and end apart: 2 -> 0, of which waited for: 2 -> 0; matrix products, arithmetic and copies ran while one was open for 0% -> 0% of each run, Pallas kernels for 0% -> 0%
where the time goes in v1:
time: 98.2 us; the launch traced here: 98.1 us
  Pallas kernels  95.8 us (98%)
  local copies, waits for them, and re-layouts  2.26 us (2%)
    pallas_call x1, Pallas kernels, per_device(): pl.pallas_call(functools.partial(body, cfg), out_shape=jax.ShapeDtypeStru...  95.8 us
    unnamed x1, local copies, waits for them, and re-layouts  2.26 us

profile of v1, /device:TPU:0, one launch (start us, length us, event | category | flops | bytes accessed | tf_op | source)
XLA Modules:
  0.0 98.1 jit_solution(14909634791088880853)
XLA Ops:
  0.0 95.8 %shard_map.46 = f32[2048,128]{1,0:T(8,128)} custom-call(f32[4096,384]{1,0:T(8,128)} %pts_ref.1, s32[1,4096]{1,0:T(1,128)} %bitcast.1, f32[2048,384]{1,0:T(8,128)} %lmk_ref.1, f32[2048,128]{1,0:T(8,128)} %coef_ref.1), custom_call_target="tpu_custom_call" | custom-call | tf_op jit(solution)/shard_map/pallas_call | solution.py:235
  95.8 2.3 %copy.6 = f32[2048,128]{1,0:T(8,128)} copy(f32[2048,128]{1,0:T(8,128)} %shard_map.46) | data formatting | bytes 2097152

commit v2 on v1

--- a/solution.py
+++ b/solution.py
@@ -117,7 +117,7 @@
             else:
                 logit[here, :] = total
 
-    def forward(chunk):
+    def split_points(chunk):
         r = pl.ds(pl.multiple_of(chunk * rows, rows), rows)
         x = pts_ref[r, :]
         hi, lo = halves(x)
@@ -126,8 +126,14 @@
         ps[:, 2 * feats:3 * feats] = hi
         norm = jnp.sum(x * x, axis=1, keepdims=True) * (-LOG2E / feats)
         ps[:, 3 * feats:] = extra_columns(norm, 0)
-        total = None
-        for j in range(m // tile):
+
+    def forward(chunk, part):
+        if part == 0:
+            split_points(chunk)
+        r = pl.ds(pl.multiple_of(chunk * rows, rows), rows)
+        total = None if part == 0 else logit[r, :]
+        tiles = m // tile
+        for j in range(part * tiles // 2, (part + 1) * tiles // 2):
             c = slice(j * tile, (j + 1) * tile)
             k = jnp.exp2(dot_nt(ps[...], ls[c, :]))
             hi, lo = halves(k)
@@ -151,30 +157,33 @@
             g = dot(both, kh[r, c])
             acc[:, c] += g[:classes] + g[classes:] + dot(hi, kl[r, c])
 
-    start_back = max(chunks, stages + 1)
+    start_back = chunks + max(0, stages // 2 - (chunks - 1) // 2)
 
     def step(t, _):
-        for s in range(stages, -1, -1):
-            chunk = t - 1 - s
-
-            @pl.when((chunk >= 0) & (chunk < chunks))
+        for part in range(2):
+            for s in range(stages, -1, -1):
+                if s % 2 != part:
+                    continue
+                chunk = t - 1 - s // 2
+
+                @pl.when((chunk >= 0) & (chunk < chunks))
+                def _():
+                    if s > 0:
+                        finish(s - 1, chunk)
+                    if s < stages:
+                        exchange(s, chunk).start()
+
+            @pl.when(t < chunks)
             def _():
-                if s > 0:
-                    finish(s - 1, chunk)
-                if s < stages:
-                    exchange(s, chunk).start()
-
-        @pl.when(t < chunks)
-        def _():
-            forward(t)
-
-        @pl.when(t >= start_back)
-        def _():
-            backward(t - start_back)
+                forward(t, part)
+
+            @pl.when(t >= start_back)
+            def _():
+                backward(2 * (t - start_back) + part)
 
         return 0
 
-    lax.fori_loop(0, start_back + chunks, step, 0)
+    lax.fori_loop(0, start_back + chunks // 2, step, 0)
 
     for j in range(m // tile):
         c = slice(j * tile, (j + 1) * tile)

time: 98.2 us -> 118 us (1.20)
  Pallas kernels: 95.8 us -> 116 us
    pallas_call x1, Pallas kernels: 95.8 us -> 116 us  [per_device(): pl.pallas_call(functools.partial(body, cfg), out_shape=jax.ShapeDtypeStru...]
where the time goes in v2:
time: 118 us
  Pallas kernels  116 us (98%)
  local copies, waits for them, and re-layouts  2.26 us (2%)
    pallas_call x1, Pallas kernels, per_device(): pl.pallas_call(functools.partial(body, cfg), out_shape=jax.ShapeDtypeStru...  116 us

profile of v2, /device:TPU:0, one launch (start us, length us, event | category | flops | bytes accessed | tf_op | source)
XLA Modules:
  0.0 117.8 jit_solution(90671690773653817)
XLA Ops:
  0.0 115.6 %shard_map.46 = f32[2048,128]{1,0:T(8,128)} custom-call(f32[4096,384]{1,0:T(8,128)} %pts_ref.1, s32[1,4096]{1,0:T(1,128)} %bitcast.1, f32[2048,384]{1,0:T(8,128)} %lmk_ref.1, f32[2048,128]{1,0:T(8,128)} %coef_ref.1), custom_call_target="tpu_custom_call" | custom-call | tf_op jit(solution)/shard_map/pallas_call | solution.py:244
  115.6 2.3 %copy.6 = f32[2048,128]{1,0:T(8,128)} copy(f32[2048,128]{1,0:T(8,128)} %shard_map.46) | data formatting | bytes 2097152
